TPU v7x, 128 devices: a whole 4x4x4 slice. The times are simulated.
128 devices in a mesh: cluster: 8 (over x, core), row: 16 (over z, y).
Axes of the slice: x: 4, y: 4, z: 4, core: 2. Of those that a mesh axis runs over, the one named last changes fastest.
Arguments:
- sources: bfloat16 [32768, 512], P(('cluster', 'row')), may hold values from -12 to 12
- targets: bfloat16 [32768, 512], P(('cluster', 'row')), may hold values from -12 to 12
- source_order: int32 [32768], P(('cluster', 'row')), may hold values from 0 to 255, as said below
- target_order: int32 [32768], P(('cluster', 'row')), may hold values from 0 to 255, as said below
Outputs:
- source_map: bfloat16 [32768, 512], P(('cluster', 'row'))
- target_map: bfloat16 [32768, 512], P(('cluster', 'row'))
Inputs may be any that keep to these rules, and one draw needn't show every extreme that they name: `source_order`: in each aligned block of 256 consecutive rows every value appears exactly once, so each block holds 32 source rows of every co-cluster. `target_order`: in each aligned block of 256 consecutive rows every value appears exactly once, so each block holds 32 target rows of every co-cluster.
All inputs are finite; a program needn't handle non-finite values.
Results may differ from a plain program's by a relative error of at most 0.01.
Values may be sent and summed in bfloat16 or wider, within the bound.
No kernel may reach another device: no remote copies, remote signals or barrier semaphores. Data moves between devices by JAX's collectives and lax.ppermute only.
A program may use at most 64 MiB of HBM per device.

v0:
```python
import math
import jax
import jax.numpy as jnp
from jax import lax
from jax.sharding import PartitionSpec as P

ITERS = 3
entropy_weight = 0.02


def square_sums(matrix):
    widened = matrix.astype(jnp.float32)
    return jnp.sum(widened * widened, axis=1)


def cost_panel(source_rows, source_norms, target_rows, target_norms):
    inner = jnp.einsum("id,jd->ij", source_rows, target_rows, preferred_element_type=jnp.float32)
    return (source_norms[:, None] + target_norms[None, :] - 2.0 * inner) / source_rows.shape[1]


def into_slots(ordering, matrix):
    positions = jnp.arange(matrix.shape[0], dtype=jnp.int32)
    selector = (positions[:, None] == ordering[None, :]).astype(jnp.bfloat16)
    return jnp.dot(selector, matrix, preferred_element_type=jnp.float32).astype(jnp.bfloat16)


def out_of_slots(ordering, matrix):
    positions = jnp.arange(matrix.shape[0], dtype=jnp.int32)
    selector = (ordering[:, None] == positions[None, :]).astype(jnp.bfloat16)
    return jnp.dot(selector, matrix, preferred_element_type=jnp.float32).astype(jnp.bfloat16)


def shards(sources, targets, source_order, target_order):
    rows_dev = sources.shape[0]
    width = sources.shape[1]
    sent_sources = into_slots(source_order, sources)
    sent_targets = into_slots(target_order, targets)
    local_sources, local_targets = (
        lax.all_to_all(sent_sources, "cluster", split_axis=0, concat_axis=0, tiled=True),
        lax.all_to_all(sent_targets, "cluster", split_axis=0, concat_axis=0, tiled=True),
    )
    cluster_targets = lax.all_gather(local_targets, "row", axis=0, tiled=True)
    columns = cluster_targets.shape[0]
    span = 512
    pieces = columns // span
    target_norms = square_sums(cluster_targets)
    target_blocks = cluster_targets.reshape(pieces, span, width)
    norm_blocks = target_norms.reshape(pieces, span)
    source_norms = square_sums(local_sources)
    log_mass = -math.log(columns)

    def row_lse(potential):

        def row_advance(carry, item):
            running, totals = carry
            block, block_norms, block_potential = item
            scores = (
                block_potential[None, :]
                - cost_panel(local_sources, source_norms, block, block_norms)
            ) / entropy_weight
            highest = jnp.maximum(running, jnp.max(scores, axis=1))
            totals = totals * jnp.exp(running - highest) + jnp.sum(
                jnp.exp(scores - highest[:, None]), axis=1
            )
            return ((highest, totals), None)

        start = (jnp.full((rows_dev,), -jnp.inf, jnp.float32), jnp.zeros((rows_dev,), jnp.float32))
        (running, totals), unused = lax.scan(
            row_advance, start, (target_blocks, norm_blocks, potential.reshape(pieces, span))
        )
        return running + jnp.log(totals)

    def column_lse(source_potential):

        def column_advance(carry, item):
            block, block_norms = item
            scores = (
                source_potential[:, None]
                - cost_panel(local_sources, source_norms, block, block_norms)
            ) / entropy_weight
            highest = jnp.max(scores, axis=0)
            return (carry, (highest, jnp.sum(jnp.exp(scores - highest[None, :]), axis=0)))

        unused, (peaks, totals) = lax.scan(column_advance, 0, (target_blocks, norm_blocks))
        peaks = peaks.reshape(-1)
        totals = totals.reshape(-1)
        highest = lax.pmax(peaks, "row")
        summed = lax.psum(totals * jnp.exp(peaks - highest), "row")
        return highest + jnp.log(summed)

    target_potential = jnp.zeros((columns,), jnp.float32)
    for repeat in range(ITERS):
        source_potential = entropy_weight * (log_mass - row_lse(target_potential))
        column_norm = column_lse(source_potential)
        target_potential = entropy_weight * (log_mass - column_norm)
    block = cluster_targets
    block_norms = target_norms
    scores = (
        source_potential[:, None] - cost_panel(local_sources, source_norms, block, block_norms)
    ) / entropy_weight
    weights = jnp.exp(scores - column_norm[None, :]).astype(jnp.bfloat16)
    target_map = lax.psum_scatter(
        jnp.einsum("ij,id->jd", weights, local_sources, preferred_element_type=jnp.float32).astype(
            jnp.bfloat16
        ),
        "row",
        scatter_dimension=0,
        tiled=True,
    )
    row_norm = row_lse(target_potential)

    def accumulate(carry, item):
        block, block_norms, block_potential = item
        scores = (
            block_potential[None, :] - cost_panel(local_sources, source_norms, block, block_norms)
        ) / entropy_weight
        weights = jnp.exp(scores - row_norm[:, None]).astype(jnp.bfloat16)
        return (carry + jnp.dot(weights, block, preferred_element_type=jnp.float32), None)

    source_sums, unused = lax.scan(
        accumulate,
        jnp.zeros((rows_dev, width), jnp.float32),
        (target_blocks, norm_blocks, target_potential.reshape(pieces, span)),
    )
    source_map = source_sums.astype(jnp.bfloat16)
    back_sources, back_targets = (
        lax.all_to_all(source_map, "cluster", split_axis=0, concat_axis=0, tiled=True),
        lax.all_to_all(target_map, "cluster", split_axis=0, concat_axis=0, tiled=True),
    )
    return (out_of_slots(source_order, back_sources), out_of_slots(target_order, back_targets))


def solution(mesh):
    return jax.shard_map(
        shards,
        mesh=mesh,
        in_specs=(
            P(("cluster", "row"), None),
            P(("cluster", "row"), None),
            P(("cluster", "row")),
            P(("cluster", "row")),
        ),
        out_specs=(P(("cluster", "row"), None), P(("cluster", "row"), None)),
        check_vma=False,
    )
```

profile of v0, /device:TPU:1, one launch (start us, length us, event | category | flops | bytes accessed | tf_op | source)
XLA Modules:
  0.0 678.2 jit_solution(1268138748987792291)
XLA Ops:
  9.0 12.2 %all_to_all.48 = bf16[8,32,512]{2,1,0:T(8,128)(2,1)} all-to-all(bf16[8,32,512]{2,1,0:T(8,128)(2,1)S(1)} %bitcast.260), channel_id=1, replica_groups=mesh['cluster'=8,'row'=16] {'cluster'}, dimensions={0} | all-to-all | bytes 524288 | tf_op jit(solution)/shard_map/all_to_all | solution.py:40
  21.2 1.9 convolution_convert_fusion.4
  23.1 4.4 all-to-all-start
  27.6 6.4 all-to-all-done
  34.2 39.4 %all-gather.2.cloned.1.call-done = bf16[4096,512]{1,0:T(8,128)(2,1)} async-done(((bf16[256,512]{1,0:T(8,128)(2,1)}), bf16[4096,512]{1,0:T(8,128)(2,1)}) %all-gather.2.cloned.1.call-update) | async-done | bytes 4194320 | tf_op jit(solution)/shard_map/all_gather | solution.py:42
  73.6 3.1 multiply_reduce_fusion
  76.7 12.7 %while.102 = (s32[]{:T(128)}, f32[256]{0:T(256)S(1)}, f32[256]{0:T(256)S(1)}, f32[256]{0:T(256)S(1)}, f32[8,512]{1,0:T(8,128)S(1)}, /*index=5*/bf16[8,512,512]{2...) while((s32[]{:T(128)}, f32[256]{0:T(256)S(1)}, f32[256]{0:T(256)S(1)}, ...), condition=%wide.region_5.6_spmd.clone, body=%wide.region_2.5_spmd.clone.sunk | while | flops 135398656 | bytes 1856108 | solution.py:68
  89.5 13.7 %while.99 = (s32[]{:T(128)}, f32[8,512]{1,0:T(8,128)S(1)}, f32[8,512]{1,0:T(8,128)S(1)}, f32[256]{0:T(256)S(1)}, f32[256]{0:T(256)S(1)}, /*index=5*/f32[8,512]{1...) while((s32[]{:T(128)}, f32[8,512]{1,0:T(8,128)S(1)}, ...), condition=%wide.region_9.10_spmd, body=%wide.region_6.9_spmd.sunk | while | flops 135396352 | bytes 1858161 | solution.py:84
  89.5 1.4 fusion.151
  91.2 1.4 fusion.151
  92.9 1.4 fusion.151
  94.6 1.4 fusion.151
  96.4 1.4 fusion.151
  98.1 1.4 fusion.151
  99.8 1.4 fusion.151
  101.5 1.4 fusion.151
  103.2 58.3 %pmax.21 = f32[4096]{0:T(1024)S(1)} all-reduce(f32[4096]{0:T(1024)S(1)} %bitcast.268), channel_id=1, replica_groups=mesh['cluster'=8,'row'=16] {'row'}, use_global_device_ids=true, to_apply=%region_10.11 | all-reduce | flops 4096 | bytes 32768 | tf_op jit(solution)/shard_map/pmax | solution.py:87
  161.5 55.6 %psum.21 = f32[4096]{0:T(1024)S(1)} all-reduce(f32[4096]{0:T(1024)S(1)} %exponential_multiply_fusion.2), channel_id=1, replica_groups=mesh['cluster'=8,'row'=16] {'row'}, use_global_device_ids=true, to_apply=%region_11.12 | all-reduce | flops 4096 | bytes 32768 | tf_op jit(solution)/shard_map/psum | solution.py:88
  217.1 12.8 %while.103 = (s32[]{:T(128)}, f32[256]{0:T(256)S(1)}, f32[256]{0:T(256)S(1)}, f32[8,512]{1,0:T(8,128)S(1)}, f32[256]{0:T(256)S(1)}, /*index=5*/f32[8,512]{1,0:T(...) while((s32[]{:T(128)}, f32[256]{0:T(256)S(1)}, ...), condition=%wide.region_15.16_spmd.clone, body=%wide.region_12.15_spmd.clone.sunk | while | flops 135398656 | bytes 1862260 | solution.py:68
  217.2 1.4 fusion.161
  218.8 1.4 fusion.161
  223.6 1.4 fusion.161
  228.4 1.4 fusion.161
  230.0 13.7 %while.100 = (s32[]{:T(128)}, f32[8,512]{1,0:T(8,128)S(1)}, f32[8,512]{1,0:T(8,128)S(1)}, f32[256]{0:T(256)S(1)}, f32[256]{0:T(256)S(1)}, /*index=5*/f32[8,512]{...) while((s32[]{:T(128)}, f32[8,512]{1,0:T(8,128)S(1)}, ...), condition=%wide.region_19.20_spmd, body=%wide.region_16.19_spmd.sunk | while | flops 135396352 | bytes 1858161 | solution.py:84
  230.0 1.4 fusion.153
  231.7 1.4 fusion.153
  233.5 1.4 fusion.153
  235.2 1.4 fusion.153
  236.9 1.4 fusion.153
  238.6 1.4 fusion.153
  240.3 1.4 fusion.153
  242.0 1.4 fusion.153
  243.7 55.6 %pmax.22 = f32[4096]{0:T(1024)S(1)} all-reduce(f32[4096]{0:T(1024)S(1)} %bitcast.270), channel_id=1, replica_groups=mesh['cluster'=8,'row'=16] {'row'}, use_global_device_ids=true, to_apply=%region_20.21 | all-reduce | flops 4096 | bytes 32768 | tf_op jit(solution)/shard_map/pmax | solution.py:87
  299.4 56.0 %psum.22 = f32[4096]{0:T(1024)S(1)} all-reduce(f32[4096]{0:T(1024)S(1)} %exponential_multiply_fusion.1), channel_id=1, replica_groups=mesh['cluster'=8,'row'=16] {'row'}, use_global_device_ids=true, to_apply=%region_21.22 | all-reduce | flops 4096 | bytes 32768 | tf_op jit(solution)/shard_map/psum | solution.py:88
  355.3 12.8 %while.104 = (s32[]{:T(128)}, f32[256]{0:T(256)S(1)}, f32[256]{0:T(256)S(1)}, f32[8,512]{1,0:T(8,128)S(1)}, f32[256]{0:T(256)S(1)}, /*index=5*/f32[8,512]{1,0:T(...) while((s32[]{:T(128)}, f32[256]{0:T(256)S(1)}, ...), condition=%wide.region_25.26_spmd.clone, body=%wide.region_22.25_spmd.clone.sunk | while | flops 135398656 | bytes 1862260 | solution.py:68
  361.8 1.4 fusion.165
  368.2 13.7 %while.101 = (s32[]{:T(128)}, f32[8,512]{1,0:T(8,128)S(1)}, f32[8,512]{1,0:T(8,128)S(1)}, f32[256]{0:T(256)S(1)}, f32[256]{0:T(256)S(1)}, /*index=5*/f32[8,512]{...) while((s32[]{:T(128)}, f32[8,512]{1,0:T(8,128)S(1)}, ...), condition=%wide.region_29.30_spmd, body=%wide.region_26.29_spmd.sunk | while | flops 135396352 | bytes 1858161 | solution.py:84
  368.2 1.4 fusion.155
  369.9 1.4 fusion.155
  371.7 1.4 fusion.155
  373.4 1.4 fusion.155
  375.1 1.4 fusion.155
  376.8 1.4 fusion.155
  378.5 1.4 fusion.155
  380.3 1.4 fusion.155
  382.0 55.6 %pmax.23 = f32[4096]{0:T(1024)S(1)} all-reduce(f32[4096]{0:T(1024)S(1)} %bitcast.272), channel_id=1, replica_groups=mesh['cluster'=8,'row'=16] {'row'}, use_global_device_ids=true, to_apply=%region_30.31 | all-reduce | flops 4096 | bytes 32768 | tf_op jit(solution)/shard_map/pmax | solution.py:87
  437.6 55.6 %psum.23 = f32[4096]{0:T(1024)S(1)} all-reduce(f32[4096]{0:T(1024)S(1)} %exponential_multiply_fusion), channel_id=1, replica_groups=mesh['cluster'=8,'row'=16] {'row'}, use_global_device_ids=true, to_apply=%region_31.32 | all-reduce | flops 4096 | bytes 32768 | tf_op jit(solution)/shard_map/psum | solution.py:88
  493.2 7.0 %convolution_convert_fusion = bf16[4096,512]{1,0:T(8,128)(2,1)} fusion(bf16[256,512]{1,0:T(8,128)(2,1)S(1)} %get-tuple-element.1322, bf16[4096,512]{1,0:T(8,128)(2,1)} %bitcast.254, f32[4096]{0:T(1024)S(1)} %get-tuple-element.614, f32[4096]{0:T(1024)S(1)} %multiply_reduce_fusion, f32[256]{0:T(256)S(1)} %get-tuple-element.1343, f32[256]{0:T(256)S(1)} %get-tuple-element.1345), kind=kOutput, calls=%fused_computation.123 | convolution fusion | flops 2157969408 | bytes 8685568 | tf_op jit(solution)/shard_map/ij,id->jd/dot_general | solution.py:103
  500.2 12.8 %while.105 = (s32[]{:T(128)}, f32[256]{0:T(256)S(1)}, f32[256]{0:T(256)S(1)}, f32[8,512]{1,0:T(8,128)S(1)}, f32[256]{0:T(256)S(1)}, /*index=5*/f32[8,512]{1,0:T(...) while((s32[]{:T(128)}, f32[256]{0:T(256)S(1)}, ...), condition=%wide.region_35.36_spmd.clone, body=%wide.region_32.35_spmd.clone.sunk | while | flops 135398656 | bytes 1862260 | solution.py:68
  503.5 1.4 fusion.169
  508.3 1.4 fusion.169
  513.1 15.4 %while.106 = (s32[]{:T(128)}, f32[256,512]{1,0:T(8,128)S(1)}, f32[8,512]{1,0:T(8,128)S(1)}, f32[256]{0:T(256)S(1)}, f32[8,512]{1,0:T(8,128)S(1)}, /*index=5*/bf1...) while((s32[]{:T(128)}, f32[256,512]{1,0:T(8,128)S(1)}, ...), condition=%wide.region_37.38_spmd.clone, body=%wide.region_36.37_spmd.clone.sunk | while | flops 269746176 | bytes 2374771 | solution.py:120
  513.1 1.9 convolution_add_fusion.2
  515.1 1.9 convolution_add_fusion.2
  517.0 1.9 convolution_add_fusion.2
  518.9 1.9 convolution_add_fusion.2
  520.8 1.9 convolution_add_fusion.2
  522.7 1.9 convolution_add_fusion.2
  524.7 1.9 convolution_add_fusion.2
  526.6 1.9 convolution_add_fusion.2
  528.5 94.9 %all_to_all.49 = bf16[8,32,512]{2,1,0:T(8,128)(2,1)S(1)} all-to-all(bf16[8,32,512]{2,1,0:T(8,128)(2,1)S(1)} %bitcast.255), channel_id=1, replica_groups=mesh['cluster'=8,'row'=16] {'cluster'}, dimensions={0} | all-to-all | bytes 524288 | tf_op jit(solution)/shard_map/all_to_all | solution.py:127
  623.4 33.8 %reduce-scatter.2.cloned.1.call-done = bf16[256,512]{1,0:T(8,128)(2,1)} async-done(((bf16[4096,512]{1,0:T(8,128)(2,1)}), bf16[256,512]{1,0:T(8,128)(2,1)}) %reduce-scatter.2.cloned.1.call-update) | async-done | bytes 262160 | tf_op jit(solution)/shard_map/reduce_scatter | solution.py:102
  657.2 6.7 all-to-all-start.3
  664.9 5.5 all-to-all-done.3
  (340 shorter events, 50.0 us)
Async XLA Ops:
  7.2 1.0 copy-start
  7.2 66.4 %all-gather.2.cloned.1.call-start = ((), (), s32[]{:S(2)}) async-start(), calls=%async_computation.5 | async-start | bytes 4456448 | tf_op jit(solution)/shard_map/all_gather | solution.py:42
  23.1 10.8 %all-to-all-start = ((bf16[8,32,512]{2,1,0:T(8,128)(2,1)}), bf16[8,32,512]{2,1,0:T(8,128)(2,1)S(1)}, u32[]{:S(2)}, u32[]{:S(2)}) async-start(bf16[8,32,512]{2,1,0:T(8,128)(2,1)} %bitcast.15), calls=%async_computation | async-start | bytes 524288 | tf_op jit(solution)/shard_map/all_to_all | solution.py:39
  27.5 629.7 %reduce-scatter.2.cloned.1.call-start = ((), (), s32[]{:S(2)}) async-start(), calls=%async_computation.6 | async-start | bytes 4456448 | tf_op jit(solution)/shard_map/reduce_scatter | solution.py:102
  513.1 150.8 %copy-start.1 = (s32[256]{0:T(256)S(1)}, s32[256]{0:T(256)}, u32[]{:S(2)}) copy-start(s32[256]{0:T(256)} %param.22) | copy-start | bytes 3076
  513.1 157.3 %copy-start.2 = (s32[256]{0:T(256)S(1)}, s32[256]{0:T(256)}, u32[]{:S(2)}) copy-start(s32[256]{0:T(256)} %param.23) | copy-start | bytes 3076
  657.2 13.2 %all-to-all-start.3 = ((bf16[8,32,512]{2,1,0:T(8,128)(2,1)}), bf16[8,32,512]{2,1,0:T(8,128)(2,1)S(1)}, u32[]{:S(2)}, u32[]{:S(2)}) async-start(bf16[8,32,512]{2,1,0:T(8,128)(2,1)} %bitcast.261), calls=%async_computation.4 | async-start | bytes 524288 | tf_op jit(solution)/shard_map/all_to_all | solution.py:128
Sparse Core Ops, SparseCore 0:
  21.3 52.2 all-gather.1
  500.3 156.7 reduce-scatter.1
where the time goes:
time: 682 us; the launch traced here: 678 us
  blocking collectives  444 us (65%)
  matrix products  106 us (16%)
  waiting for transfers between devices  85.2 us (12%)
  between operations  14.3 us (2%)
  starting transfers between devices  11.1 us (2%)
  other arithmetic  10.7 us (2%)
    pmax x3, blocking collectives, column_lse(): highest = lax.pmax(peaks, 'row')  170 us
    psum x3, blocking collectives, column_lse(): summed = lax.psum(totals * jnp.exp(peaks - highest), 'row')  167 us
    all_to_all x1, blocking collectives, shards(): lax.all_to_all(source_map, 'cluster', split_axis=0, concat_axis=0, tiled=...  94.9 us
    dot_general x56, matrix products, cost_panel(): jnp.einsum('id,jd->ij', source_rows, target_rows, preferred_element_type=...  79.3 us
    all_gather x1, waiting for transfers between devices, shards(): cluster_targets = lax.all_gather(local_targets, 'row', axis=0, tiled=True)  39.4 us
    reduce_scatter x1, waiting for transfers between devices, shards(): lax.psum_scatter(jnp.einsum('ij,id->jd', weights, local_sources, preferre...  33.8 us
    dot_general x8, matrix products, accumulate(): jnp.dot(weights, block, preferred_element_type=jnp.float32)  15 us
  transfers between devices with their start and end apart: 4, of which 4 were waited for; matrix products, arithmetic and copies ran while one was open for 5% of the time, Pallas kernels for 0%

commit v1 on v0

--- a/solution.py
+++ b/solution.py
@@ -6,6 +6,25 @@
 
 ITERS = 3
 entropy_weight = 0.02
+
+
+def _remake_sample(packet, dimension_no, field):
+    moved = packet.shape
+    outcome_arr = jnp.moveaxis(
+        packet.reshape(
+            *moved[:dimension_no], field, moved[dimension_no] // field, *moved[dimension_no + 1 :]
+        ),
+        dimension_no,
+        0,
+    )
+    return outcome_arr
+
+
+def note_streams(local_values, array_dim):
+    u1 = list(local_values.shape[1:])
+    u1[array_dim] *= local_values.shape[0]
+    later = jnp.moveaxis(local_values, 0, array_dim).reshape(u1)
+    return later
 
 
 def square_sums(matrix):
@@ -123,8 +142,26 @@
         (target_blocks, norm_blocks, target_potential.reshape(pieces, span)),
     )
     source_map = source_sums.astype(jnp.bfloat16)
+
+    def sections_note(block_in, chip_axis, w_in, message):
+        value_now, wide_out = (lax.axis_size(chip_axis), lax.axis_index(chip_axis))
+        z_new = _remake_sample(block_in, w_in, value_now)
+        made = [z_new[wide_out]]
+        for dev_i in range(1, value_now):
+            current_arr = z_new[wide_out ^ dev_i]
+            made.append(
+                lax.ppermute(
+                    current_arr,
+                    axis_name=chip_axis,
+                    perm=[(b, b ^ dev_i) for b in range(value_now)],
+                )
+            )
+        z_new = jnp.stack(made, axis=0)[wide_out ^ jnp.arange(value_now)]
+        before = note_streams(z_new, message)
+        return before
+
     back_sources, back_targets = (
-        lax.all_to_all(source_map, "cluster", split_axis=0, concat_axis=0, tiled=True),
+        sections_note(source_map, "cluster", 0, 0),
         lax.all_to_all(target_map, "cluster", split_axis=0, concat_axis=0, tiled=True),
     )
     return (out_of_slots(source_order, back_sources), out_of_slots(target_order, back_targets))

time: 682 us -> 682 us (level)
  blocking collectives: 444 us -> 349 us
  starting transfers between devices: 11.1 us -> 104 us
    all_to_all x1 -> x0, blocking collectives: 94.9 us -> none  [shards(): lax.all_to_all(source_map, 'cluster', split_axis=0, concat_axis=0, tiled=...]
    ppermute x0 -> x7, starting transfers between devices: none -> 92.4 us  [sections_note(): lax.ppermute(current_arr, axis_name=chip_axis, perm=[(b, b ^ dev_i) for b...]
  transfers between devices with their start and end apart: 4 -> 11, of which waited for: 4 -> 7; matrix products, arithmetic and copies ran while one was open for 5% -> 5% of each run, Pallas kernels for 0% -> 0%
where the time goes in v1:
time: 682 us; the launch traced here: 678 us
  blocking collectives  349 us (51%)
  matrix products  106 us (16%)
  starting transfers between devices  104 us (15%)
  waiting for transfers between devices  86.9 us (13%)
  between operations  14.4 us (2%)
  other arithmetic  10.8 us (2%)
    pmax x3, blocking collectives, column_lse(): highest = lax.pmax(peaks, 'row')  170 us
    psum x3, blocking collectives, column_lse(): summed = lax.psum(totals * jnp.exp(peaks - highest), 'row')  167 us
    ppermute x7, starting transfers between devices, sections_note(): lax.ppermute(current_arr, axis_name=chip_axis, perm=[(b, b ^ dev_i) for b...  92.4 us
    dot_general x56, matrix products, cost_panel(): jnp.einsum('id,jd->ij', source_rows, target_rows, preferred_element_type=...  79.3 us
    all_gather x1, waiting for transfers between devices, shards(): cluster_targets = lax.all_gather(local_targets, 'row', axis=0, tiled=True)  39.4 us
    reduce_scatter x1, waiting for transfers between devices, shards(): lax.psum_scatter(jnp.einsum('ij,id->jd', weights, local_sources, preferre...  31.3 us
    dot_general x8, matrix products, accumulate(): jnp.dot(weights, block, preferred_element_type=jnp.float32)  15 us
  transfers between devices with their start and end apart: 11, of which 7 were waited for; matrix products, arithmetic and copies ran while one was open for 5% of the time, Pallas kernels for 0%

profile of v1, /device:TPU:1, one launch (start us, length us, event | category | flops | bytes accessed | tf_op | source)
XLA Modules:
  0.0 678.2 jit_solution(10181776148048518780)
XLA Ops:
  9.0 12.2 %all_to_all.36 = bf16[8,32,512]{2,1,0:T(8,128)(2,1)} all-to-all(bf16[8,32,512]{2,1,0:T(8,128)(2,1)S(1)} %bitcast.290), channel_id=1, replica_groups=mesh['cluster'=8,'row'=16] {'cluster'}, dimensions={0} | all-to-all | bytes 524288 | tf_op jit(solution)/shard_map/all_to_all | solution.py:59
  21.2 1.9 convolution_convert_fusion.4
  23.1 4.4 all-to-all-start
  27.6 6.4 all-to-all-done
  34.2 39.4 %all-gather.2.cloned.1.call-done = bf16[4096,512]{1,0:T(8,128)(2,1)} async-done(((bf16[256,512]{1,0:T(8,128)(2,1)}), bf16[4096,512]{1,0:T(8,128)(2,1)}) %all-gather.2.cloned.1.call-update) | async-done | bytes 4194320 | tf_op jit(solution)/shard_map/all_gather | solution.py:61
  73.6 3.1 multiply_reduce_fusion
  76.7 12.7 %while.102 = (s32[]{:T(128)}, f32[256]{0:T(256)S(1)}, f32[256]{0:T(256)S(1)}, f32[256]{0:T(256)S(1)}, f32[8,512]{1,0:T(8,128)S(1)}, /*index=5*/bf16[8,512,512]{2...) while((s32[]{:T(128)}, f32[256]{0:T(256)S(1)}, f32[256]{0:T(256)S(1)}, ...), condition=%wide.region_5.6_spmd.clone, body=%wide.region_2.5_spmd.clone.sunk | while | flops 135398656 | bytes 1856108 | solution.py:87
  89.5 13.7 %while.99 = (s32[]{:T(128)}, f32[8,512]{1,0:T(8,128)S(1)}, f32[8,512]{1,0:T(8,128)S(1)}, f32[256]{0:T(256)S(1)}, f32[256]{0:T(256)S(1)}, /*index=5*/f32[8,512]{1...) while((s32[]{:T(128)}, f32[8,512]{1,0:T(8,128)S(1)}, ...), condition=%wide.region_9.10_spmd, body=%wide.region_6.9_spmd.sunk | while | flops 135396352 | bytes 1858161 | solution.py:103
  89.5 1.4 fusion.152
  91.2 1.4 fusion.152
  92.9 1.4 fusion.152
  94.6 1.4 fusion.152
  96.4 1.4 fusion.152
  98.1 1.4 fusion.152
  99.8 1.4 fusion.152
  101.5 1.4 fusion.152
  103.2 58.3 %pmax.21 = f32[4096]{0:T(1024)S(1)} all-reduce(f32[4096]{0:T(1024)S(1)} %bitcast.298), channel_id=1, replica_groups=mesh['cluster'=8,'row'=16] {'row'}, use_global_device_ids=true, to_apply=%region_10.11 | all-reduce | flops 4096 | bytes 32768 | tf_op jit(solution)/shard_map/pmax | solution.py:106
  161.5 55.6 %psum.21 = f32[4096]{0:T(1024)S(1)} all-reduce(f32[4096]{0:T(1024)S(1)} %exponential_multiply_fusion.2), channel_id=1, replica_groups=mesh['cluster'=8,'row'=16] {'row'}, use_global_device_ids=true, to_apply=%region_11.12 | all-reduce | flops 4096 | bytes 32768 | tf_op jit(solution)/shard_map/psum | solution.py:107
  217.1 12.8 %while.103 = (s32[]{:T(128)}, f32[256]{0:T(256)S(1)}, f32[256]{0:T(256)S(1)}, f32[8,512]{1,0:T(8,128)S(1)}, f32[256]{0:T(256)S(1)}, /*index=5*/f32[8,512]{1,0:T(...) while((s32[]{:T(128)}, f32[256]{0:T(256)S(1)}, ...), condition=%wide.region_15.16_spmd.clone, body=%wide.region_12.15_spmd.clone.sunk | while | flops 135398656 | bytes 1862260 | solution.py:87
  217.2 1.4 fusion.162
  223.6 1.4 fusion.162
  228.4 1.4 fusion.162
  230.0 13.7 %while.100 = (s32[]{:T(128)}, f32[8,512]{1,0:T(8,128)S(1)}, f32[8,512]{1,0:T(8,128)S(1)}, f32[256]{0:T(256)S(1)}, f32[256]{0:T(256)S(1)}, /*index=5*/f32[8,512]{...) while((s32[]{:T(128)}, f32[8,512]{1,0:T(8,128)S(1)}, ...), condition=%wide.region_19.20_spmd, body=%wide.region_16.19_spmd.sunk | while | flops 135396352 | bytes 1858161 | solution.py:103
  230.0 1.4 fusion.154
  231.7 1.4 fusion.154
  233.5 1.4 fusion.154
  235.2 1.4 fusion.154
  236.9 1.4 fusion.154
  238.6 1.4 fusion.154
  240.3 1.4 fusion.154
  242.0 1.4 fusion.154
  243.7 55.6 %pmax.22 = f32[4096]{0:T(1024)S(1)} all-reduce(f32[4096]{0:T(1024)S(1)} %bitcast.300), channel_id=1, replica_groups=mesh['cluster'=8,'row'=16] {'row'}, use_global_device_ids=true, to_apply=%region_20.21 | all-reduce | flops 4096 | bytes 32768 | tf_op jit(solution)/shard_map/pmax | solution.py:106
  299.4 56.0 %psum.22 = f32[4096]{0:T(1024)S(1)} all-reduce(f32[4096]{0:T(1024)S(1)} %exponential_multiply_fusion.1), channel_id=1, replica_groups=mesh['cluster'=8,'row'=16] {'row'}, use_global_device_ids=true, to_apply=%region_21.22 | all-reduce | flops 4096 | bytes 32768 | tf_op jit(solution)/shard_map/psum | solution.py:107
  355.3 12.8 %while.104 = (s32[]{:T(128)}, f32[256]{0:T(256)S(1)}, f32[256]{0:T(256)S(1)}, f32[8,512]{1,0:T(8,128)S(1)}, f32[256]{0:T(256)S(1)}, /*index=5*/f32[8,512]{1,0:T(...) while((s32[]{:T(128)}, f32[256]{0:T(256)S(1)}, ...), condition=%wide.region_25.26_spmd.clone, body=%wide.region_22.25_spmd.clone.sunk | while | flops 135398656 | bytes 1862260 | solution.py:87
  368.2 13.7 %while.101 = (s32[]{:T(128)}, f32[8,512]{1,0:T(8,128)S(1)}, f32[8,512]{1,0:T(8,128)S(1)}, f32[256]{0:T(256)S(1)}, f32[256]{0:T(256)S(1)}, /*index=5*/f32[8,512]{...) while((s32[]{:T(128)}, f32[8,512]{1,0:T(8,128)S(1)}, ...), condition=%wide.region_29.30_spmd, body=%wide.region_26.29_spmd.sunk | while | flops 135396352 | bytes 1858161 | solution.py:103
  368.2 1.4 fusion.156
  369.9 1.4 fusion.156
  371.7 1.4 fusion.156
  373.4 1.4 fusion.156
  375.1 1.4 fusion.156
  376.8 1.4 fusion.156
  378.5 1.4 fusion.156
  380.3 1.4 fusion.156
  382.0 55.6 %pmax.23 = f32[4096]{0:T(1024)S(1)} all-reduce(f32[4096]{0:T(1024)S(1)} %bitcast.302), channel_id=1, replica_groups=mesh['cluster'=8,'row'=16] {'row'}, use_global_device_ids=true, to_apply=%region_30.31 | all-reduce | flops 4096 | bytes 32768 | tf_op jit(solution)/shard_map/pmax | solution.py:106
  437.6 55.6 %psum.23 = f32[4096]{0:T(1024)S(1)} all-reduce(f32[4096]{0:T(1024)S(1)} %exponential_multiply_fusion), channel_id=1, replica_groups=mesh['cluster'=8,'row'=16] {'row'}, use_global_device_ids=true, to_apply=%region_31.32 | all-reduce | flops 4096 | bytes 32768 | tf_op jit(solution)/shard_map/psum | solution.py:107
  493.2 7.0 %convolution_convert_fusion = bf16[4096,512]{1,0:T(8,128)(2,1)} fusion(bf16[256,512]{1,0:T(8,128)(2,1)S(1)} %get-tuple-element.1330, bf16[4096,512]{1,0:T(8,128)(2,1)} %bitcast.284, f32[4096]{0:T(1024)S(1)} %get-tuple-element.614, f32[4096]{0:T(1024)S(1)} %multiply_reduce_fusion, f32[256]{0:T(256)S(1)} %get-tuple-element.1365, f32[256]{0:T(256)S(1)} %get-tuple-element.1367), kind=kOutput, calls=%fused_computation.124 | convolution fusion | flops 2157969408 | bytes 8685568 | tf_op jit(solution)/shard_map/ij,id->jd/dot_general | solution.py:122
  500.2 12.8 %while.105 = (s32[]{:T(128)}, f32[256]{0:T(256)S(1)}, f32[256]{0:T(256)S(1)}, f32[8,512]{1,0:T(8,128)S(1)}, f32[256]{0:T(256)S(1)}, /*index=5*/f32[8,512]{1,0:T(...) while((s32[]{:T(128)}, f32[256]{0:T(256)S(1)}, ...), condition=%wide.region_35.36_spmd.clone, body=%wide.region_32.35_spmd.clone.sunk | while | flops 135398656 | bytes 1862260 | solution.py:87
  503.5 1.4 fusion.170
  513.1 15.4 %while.106 = (s32[]{:T(128)}, f32[256,512]{1,0:T(8,128)S(1)}, f32[8,512]{1,0:T(8,128)S(1)}, f32[256]{0:T(256)S(1)}, f32[8,512]{1,0:T(8,128)S(1)}, /*index=5*/bf1...) while((s32[]{:T(128)}, f32[256,512]{1,0:T(8,128)S(1)}, ...), condition=%wide.region_37.38_spmd.clone, body=%wide.region_36.37_spmd.clone.sunk | while | flops 269746176 | bytes 2374771 | solution.py:139
  513.1 1.9 convolution_add_fusion.2
  515.1 1.9 convolution_add_fusion.2
  517.0 1.9 convolution_add_fusion.2
  518.9 1.9 convolution_add_fusion.2
  520.8 1.9 convolution_add_fusion.2
  522.7 1.9 convolution_add_fusion.2
  524.7 1.9 convolution_add_fusion.2
  526.6 1.9 convolution_add_fusion.2
  528.6 84.5 %collective-permute-start = (bf16[32,512]{1,0:T(8,128)(2,1)S(1)}, bf16[32,512]{1,0:T(8,128)(2,1)S(1)}, u32[]{:S(2)}, u32[]{:S(2)}) collective-permute-start(bf16[32,512]{1,0:T(8,128)(2,1)S(1)} %get-tuple-element.643), channel_id=1, source_target_pairs={{0,16},{16,0},{32,48},{48,32},{64,80},{80,64},{96,112},{112,96},{1... | collective-permute-start | bytes 98312 | tf_op jit(solution)/shard_map/ppermute | solution.py:153
  614.8 2.6 collective-permute-start.3
  618.1 2.3 collective-permute-start.5
  623.3 2.0 collective-permute-done.6
  625.8 31.3 %reduce-scatter.2.cloned.1.call-done = bf16[256,512]{1,0:T(8,128)(2,1)} async-done(((bf16[4096,512]{1,0:T(8,128)(2,1)}), bf16[256,512]{1,0:T(8,128)(2,1)}) %reduce-scatter.2.cloned.1.call-update) | async-done | bytes 262160 | tf_op jit(solution)/shard_map/reduce_scatter | solution.py:121
  657.2 6.7 all-to-all-start.2
  664.9 5.5 all-to-all-done.2
  (364 shorter events, 60.1 us)
Async XLA Ops:
  7.2 1.0 copy-start
  7.2 66.4 %all-gather.2.cloned.1.call-start = ((), (), s32[]{:S(2)}) async-start(), calls=%async_computation.4 | async-start | bytes 4456448 | tf_op jit(solution)/shard_map/all_gather | solution.py:61
  23.1 10.8 %all-to-all-start = ((bf16[8,32,512]{2,1,0:T(8,128)(2,1)}), bf16[8,32,512]{2,1,0:T(8,128)(2,1)S(1)}, u32[]{:S(2)}, u32[]{:S(2)}) async-start(bf16[8,32,512]{2,1,0:T(8,128)(2,1)} %bitcast.15), calls=%async_computation | async-start | bytes 524288 | tf_op jit(solution)/shard_map/all_to_all | solution.py:58
  27.5 629.7 %reduce-scatter.2.cloned.1.call-start = ((), (), s32[]{:S(2)}) async-start(), calls=%async_computation.5 | async-start | bytes 4456448 | tf_op jit(solution)/shard_map/reduce_scatter | solution.py:121
  513.1 150.8 %copy-start.1 = (s32[256]{0:T(256)S(1)}, s32[256]{0:T(256)}, u32[]{:S(2)}) copy-start(s32[256]{0:T(256)} %param.22) | copy-start | bytes 3076
  513.1 157.3 %copy-start.2 = (s32[256]{0:T(256)S(1)}, s32[256]{0:T(256)}, u32[]{:S(2)}) copy-start(s32[256]{0:T(256)} %param.23) | copy-start | bytes 3076
  528.6 89.5 %collective-permute-start = (bf16[32,512]{1,0:T(8,128)(2,1)S(1)}, bf16[32,512]{1,0:T(8,128)(2,1)S(1)}, u32[]{:S(2)}, u32[]{:S(2)}) collective-permute-start(bf16[32,512]{1,0:T(8,128)(2,1)S(1)} %get-tuple-element.643), channel_id=1, source_target_pairs={{0,16},{16,0},{32,48},{48,32},{64,80},{80,64},{96,112},{112,96},{1... | collective-permute-start | bytes 98312 | tf_op jit(solution)/shard_map/ppermute | solution.py:153
  613.1 7.3 %collective-permute-start.1 = (bf16[32,512]{1,0:T(8,128)(2,1)S(1)}, bf16[32,512]{1,0:T(8,128)(2,1)S(1)}, u32[]{:S(2)}, u32[]{:S(2)}) collective-permute-start(bf16[32,512]{1,0:T(8,128)(2,1)S(1)} %get-tuple-element.642), channel_id=1, source_target_pairs={{0,32},{16,48},{32,0},{48,16},{64,96},{80,112},{96,64},{112,80},{1... | collective-permute-start | bytes 98312 | tf_op jit(solution)/shard_map/ppermute | solution.py:153
  614.2 6.8 %collective-permute-start.2 = (bf16[32,512]{1,0:T(8,128)(2,1)S(1)}, bf16[32,512]{1,0:T(8,128)(2,1)S(1)}, u32[]{:S(2)}, u32[]{:S(2)}) collective-permute-start(bf16[32,512]{1,0:T(8,128)(2,1)S(1)} %get-tuple-element.641), channel_id=1, source_target_pairs={{0,48},{16,32},{32,16},{48,0},{64,112},{80,96},{96,80},{112,64},{1... | collective-permute-start | bytes 98312 | tf_op jit(solution)/shard_map/ppermute | solution.py:153
  614.8 6.2 collective-permute-start.3
  617.4 5.0 collective-permute-start.4
  618.1 5.2 collective-permute-start.5
  620.4 4.8 collective-permute-start.6
  657.2 13.2 %all-to-all-start.2 = ((bf16[8,32,512]{2,1,0:T(8,128)(2,1)}), bf16[8,32,512]{2,1,0:T(8,128)(2,1)S(1)}, u32[]{:S(2)}, u32[]{:S(2)}) async-start(bf16[8,32,512]{2,1,0:T(8,128)(2,1)} %bitcast.291), calls=%async_computation.3 | async-start | bytes 524288 | tf_op jit(solution)/shard_map/all_to_all | solution.py:165
Sparse Core Ops, SparseCore 0:
  21.3 52.2 all-gather.1
  500.3 156.7 reduce-scatter.1
